TPU v7x, 32 devices: a whole 2x2x4 slice. The times are simulated.
32 devices in a mesh: blk: 8 (over z, y), tab: 4 (over x, core).
Axes of the slice: x: 2, y: 2, z: 4, core: 2. Of those that a mesh axis runs over, the one named last changes fastest.
Arguments:
- accounts: bfloat16 [65536, 128], P(('blk', 'tab')), may hold values from -0.5 to 0.5
- merchants: bfloat16 [65536, 128], P(('blk', 'tab')), may hold values from -6 to 6
- logit_scale: float32 [1], replicated, may hold values from 1 to 4
- logit_bias: float32 [1], replicated, may hold values from -3 to -1
- positive: int32 [65536], P(('blk', 'tab')), may hold values from 0 to 8191
- account_ids: int32 [65536], P(('blk', 'tab')), may hold values from 0 to 1023
- merchant_ids: int32 [65536], P(('blk', 'tab')), may hold values from 0 to 1023
- account_owner: int32 [512, 1], P(('blk', 'tab')), may hold values from 0 to 3; in each aligned block of 16 rows (0 to 15, 16 to 31, ...) at most 8 rows name the same one
- merchant_owner: int32 [512, 1], P(('blk', 'tab')), may hold values from 0 to 3; in each aligned block of 16 rows (0 to 15, 16 to 31, ...) at most 8 rows name the same one
Outputs:
- account_grad: float32 [32768, 128], P(('blk', 'tab'))
- merchant_grad: float32 [32768, 128], P(('blk', 'tab'))
Inputs may be any that keep to these rules, and one draw needn't show every extreme that they name: `account_owner`: among the 16 row blocks of one batch block at most 8 have the same owner, and some batch block gives exactly 8 to one owner. `merchant_owner`: among the 16 row blocks of one batch block at most 8 have the same owner, and some batch block gives exactly 8 to one owner.
All inputs are finite; a program needn't handle non-finite values.
Results may differ from a plain program's by a relative error of at most 0.00048.
Values may be sent and summed in bfloat16 or wider, within the bound.
A program may use at most 64 MiB of HBM per device.

v0:
```python
import jax
import jax.numpy as jnp
from jax import lax
from jax.sharding import PartitionSpec as P

D = 128
STEPS = 4
BLOCK_ROWS = 128
TROWS = 1024


def shifted(block, axis, distance):
    devices = range(lax.axis_size(axis))
    route = [((i - distance) % len(devices), i) for i in devices]
    return lax.ppermute(block, axis, route)


def score_delta(piece, label, merch_block, columns, scale, bias):
    logits = (
        scale
        * lax.dot_general(
            piece, merch_block, (((1,), (1,)), ((), ())), preferred_element_type=jnp.float32
        )
        + bias
    )
    signs = jnp.where(label[:, None] == columns[None, :], jnp.float32(1.0), jnp.float32(-1.0))
    return (-signs * jax.nn.sigmoid(-signs * logits)).astype(jnp.bfloat16)


def tile_grads(acc_block, merch_block, relative, scale, bias):
    row_count = acc_block.shape[0]
    row_step = min(512, row_count)
    count = row_count // row_step
    pieces = acc_block.reshape(count, row_step, D)
    labels = relative.reshape(count, row_step)
    columns = jnp.arange(merch_block.shape[0], dtype=jnp.int32)

    def tile_one_block(carry, item):
        piece, label = item
        delta = score_delta(piece, label, merch_block, columns, scale, bias)
        grad_rows = scale * jnp.dot(delta, merch_block, preferred_element_type=jnp.float32)
        merch_part = carry + scale * lax.dot_general(
            delta, piece, (((0,), (0,)), ((), ())), preferred_element_type=jnp.float32
        )
        return (merch_part, grad_rows)

    start = jnp.zeros((merch_block.shape[0], D), jnp.float32)
    merch_grad, acc_grad = lax.scan(tile_one_block, start, (pieces, labels))
    return (acc_grad.reshape(-1, D), merch_grad)


def account_only(acc_block, merch_block, relative, offset, scale, bias):
    row_count = acc_block.shape[0]
    row_step = min(512, row_count)
    count = row_count // row_step
    pieces = acc_block.reshape(count, row_step, D)
    labels = relative.reshape(count, row_step)
    columns = offset + jnp.arange(merch_block.shape[0], dtype=jnp.int32)

    def account_one_block(item):
        piece, label = item
        delta = score_delta(piece, label, merch_block, columns, scale, bias)
        return scale * jnp.dot(delta, merch_block, preferred_element_type=jnp.float32)

    return lax.map(account_one_block, (pieces, labels)).reshape(-1, D)


def merchant_only(acc_block, merch_block, relative, offset, scale, bias):
    row_count = acc_block.shape[0]
    row_step = min(512, row_count)
    count = row_count // row_step
    pieces = acc_block.reshape(count, row_step, D)
    labels = relative.reshape(count, row_step)
    columns = offset + jnp.arange(merch_block.shape[0], dtype=jnp.int32)

    def merchant_one_block(carry, item):
        piece, label = item
        delta = score_delta(piece, label, merch_block, columns, scale, bias)
        return (
            carry
            + scale
            * lax.dot_general(
                delta, piece, (((0,), (0,)), ((), ())), preferred_element_type=jnp.float32
            ),
            None,
        )

    start = jnp.zeros((merch_block.shape[0], D), jnp.float32)
    merch_grad, unused = lax.scan(merchant_one_block, start, (pieces, labels))
    return merch_grad


def pack_blocks(grads, ids, owner, owners_count):
    owner_list = owner[:, 0]
    block_count = owner_list.shape[0]
    capacity = block_count // 2
    lanes = jnp.arange(owners_count, dtype=jnp.int32)
    hitting = (owner_list[:, None] == lanes[None, :]).astype(jnp.int32)
    earlier = jnp.cumsum(hitting, axis=0) - hitting
    ranking = jnp.sum(earlier * hitting, axis=1)
    placing = owner_list * capacity + ranking
    slots = jnp.arange(owners_count * capacity, dtype=jnp.int32)
    matching = placing[None, :] == slots[:, None]
    filled = jnp.any(matching, axis=1)
    source = jnp.argmax(matching, axis=1)
    payload = jnp.take(grads.reshape(block_count, BLOCK_ROWS, D), source, axis=0)
    payload = jnp.where(filled[:, None, None], payload, jnp.float32(0.0))
    row_keys = jnp.take(ids.reshape(block_count, BLOCK_ROWS), source, axis=0)
    row_keys = jnp.where(filled[:, None], row_keys, 0)
    return (
        payload.reshape(owners_count, capacity, BLOCK_ROWS, D),
        row_keys.reshape(owners_count, capacity, BLOCK_ROWS),
    )


def per_device(
    accounts,
    merchants,
    logit_scale,
    logit_bias,
    positive,
    account_ids,
    merchant_ids,
    account_owner,
    merchant_owner,
):
    scale = logit_scale[0]
    bias = logit_bias[0]
    row_count = accounts.shape[0]
    acc_grad, merch_grad = tile_grads(accounts, merchants, positive, scale, bias)
    visiting = merchants
    guest_rows = accounts
    guest_labels = positive
    for cycle_step in range(1, STEPS):
        visiting = shifted(visiting, "blk", 1)
        guest_rows, guest_labels = shifted((guest_rows, guest_labels), "blk", -1)
        acc_grad = acc_grad + account_only(
            accounts, visiting, positive, cycle_step * row_count, scale, bias
        )
        merch_grad = merch_grad + merchant_only(
            guest_rows, merchants, guest_labels, cycle_step * row_count, scale, bias
        )
    owners_count = lax.axis_size("tab")
    acc_payload, acc_keys = pack_blocks(acc_grad, account_ids, account_owner, owners_count)
    merch_payload, merch_keys = pack_blocks(merch_grad, merchant_ids, merchant_owner, owners_count)
    acc_payload, acc_keys, merch_payload, merch_keys = (
        lax.all_to_all(acc_payload, "tab", split_axis=0, concat_axis=0, tiled=True),
        lax.all_to_all(acc_keys, "tab", split_axis=0, concat_axis=0, tiled=True),
        lax.all_to_all(merch_payload, "tab", split_axis=0, concat_axis=0, tiled=True),
        lax.all_to_all(merch_keys, "tab", split_axis=0, concat_axis=0, tiled=True),
    )
    account_grad = jax.ops.segment_sum(
        acc_payload.reshape(-1, D), acc_keys.reshape(-1), num_segments=TROWS
    )
    merchant_grad = jax.ops.segment_sum(
        merch_payload.reshape(-1, D), merch_keys.reshape(-1), num_segments=TROWS
    )
    return (account_grad, merchant_grad)


def solution(mesh):
    return jax.shard_map(
        per_device,
        mesh=mesh,
        in_specs=(
            P(("blk", "tab"), None),
            P(("blk", "tab"), None),
            P(),
            P(),
            P(("blk", "tab")),
            P(("blk", "tab")),
            P(("blk", "tab")),
            P(("blk", "tab"), None),
            P(("blk", "tab"), None),
        ),
        out_specs=(P(("blk", "tab"), None), P(("blk", "tab"), None)),
        check_vma=False,
    )
```

profile of v0, /device:TPU:0, one launch (start us, length us, event | category | flops | bytes accessed | tf_op | source)
XLA Modules:
  0.0 283.2 jit_solution(10152062335800458966)
XLA Ops:
  18.8 37.1 %while.82 = (s32[]{:T(128)}, f32[2048,128]{1,0:T(8,128)S(1)}, f32[4,512,128]{2,1,0:T(8,128)}, f32[]{:T(128)}, s32[4,512]{1,0:T(4,128)S(1)}, /*index=5*/bf16[4,51...) while((s32[]{:T(128)}, f32[2048,128]{1,0:T(8,128)S(1)}, ...), condition=%wide.region_5.7_spmd.clone, body=%wide.region_4.6_spmd.clone.sunk | while | flops 817692672 | bytes 12068495 | solution.py:48
  66.7 20.7 %while.83 = (s32[]{:T(128)}, f32[2048,128]{1,0:T(8,128)S(1)}, f32[]{:T(128)}, s32[4,512]{1,0:T(4,128)S(1)}, bf16[4,512,128]{2,1,0:T(8,128)(2,1)}, /*index=5*/bf1...) while((s32[]{:T(128)}, f32[2048,128]{1,0:T(8,128)S(1)}, f32[]{:T(128)}, ...), condition=%wide.region_18.21_spmd.clone, body=%wide.region_17.20_spmd.clone.sunk | while | flops 549193728 | bytes 2908779 | solution.py:89
  66.8 5.2 %fusion.164 = f32[2048,128]{1,0:T(8,128)S(1)} fusion(bf16[2048,128]{1,0:T(8,128)(2,1)} %get-tuple-element.1057, f32[]{:T(128)} %get-tuple-element.1058, f32[]{:T(128)} %get-tuple-element.1054, s32[2048]{0:T(1024)S(1)} %iota_add_fusion.15, s32[512]{0:T(512)S(1)} %bitcast.165, f32[2048,128]{1,0:T(8,128)S(1)} %get-tuple-element.1044, ...), kind=kOutput, calls=%fused_computation.65.clone.1 | convolution fusion | flops 549191680 | bytes 2896385 | tf_op jit(solution)/shard_map/while/body/eval_jaxpr/dot_general | solution.py:82
  72.0 5.1 %fusion.164 = f32[2048,128]{1,0:T(8,128)S(1)} fusion(bf16[2048,128]{1,0:T(8,128)(2,1)} %get-tuple-element.1057, f32[]{:T(128)} %get-tuple-element.1058, f32[]{:T(128)} %get-tuple-element.1054, s32[2048]{0:T(1024)S(1)} %iota_add_fusion.15, s32[512]{0:T(512)S(1)} %bitcast.165, f32[2048,128]{1,0:T(8,128)S(1)} %get-tuple-element.1044, ...), kind=kOutput, calls=%fused_computation.65.clone.1 | convolution fusion | flops 549191680 | bytes 2896385 | tf_op jit(solution)/shard_map/while/body/eval_jaxpr/dot_general | solution.py:82
  77.1 5.1 %fusion.164 = f32[2048,128]{1,0:T(8,128)S(1)} fusion(bf16[2048,128]{1,0:T(8,128)(2,1)} %get-tuple-element.1057, f32[]{:T(128)} %get-tuple-element.1058, f32[]{:T(128)} %get-tuple-element.1054, s32[2048]{0:T(1024)S(1)} %iota_add_fusion.15, s32[512]{0:T(512)S(1)} %bitcast.165, f32[2048,128]{1,0:T(8,128)S(1)} %get-tuple-element.1044, ...), kind=kOutput, calls=%fused_computation.65.clone.1 | convolution fusion | flops 549191680 | bytes 2896385 | tf_op jit(solution)/shard_map/while/body/eval_jaxpr/dot_general | solution.py:82
  82.3 5.1 %fusion.164 = f32[2048,128]{1,0:T(8,128)S(1)} fusion(bf16[2048,128]{1,0:T(8,128)(2,1)} %get-tuple-element.1057, f32[]{:T(128)} %get-tuple-element.1058, f32[]{:T(128)} %get-tuple-element.1054, s32[2048]{0:T(1024)S(1)} %iota_add_fusion.15, s32[512]{0:T(512)S(1)} %bitcast.165, f32[2048,128]{1,0:T(8,128)S(1)} %get-tuple-element.1044, ...), kind=kOutput, calls=%fused_computation.65.clone.1 | convolution fusion | flops 549191680 | bytes 2896385 | tf_op jit(solution)/shard_map/while/body/eval_jaxpr/dot_general | solution.py:82
  87.4 5.0 %collective-permute-start.6 = (bf16[2048,128]{1,0:T(8,128)(2,1)}, bf16[2048,128]{1,0:T(8,128)(2,1)}, u32[]{:S(2)}, u32[]{:S(2)}) collective-permute-start(bf16[2048,128]{1,0:T(8,128)(2,1)} %collective-permute-done.4), channel_id=1, source_target_pairs={{4,0},{8,4},{12,8},{16,12},{20,16},{24,20},{28,24},{0,28},{5,1},{9... | collective-permute-start | bytes 1572872 | tf_op jit(solution)/shard_map/ppermute | solution.py:15
  92.6 18.2 %while.79 = (s32[]{:T(128)}, f32[4,512,128]{2,1,0:T(8,128)S(1)}, f32[]{:T(128)}, s32[4,512]{1,0:T(4,128)S(1)}, bf16[4,512,128]{2,1,0:T(8,128)(2,1)S(1)}, /*index=5*/bf16[2048,128]{1,0:T(8,128)(2,1)}, f32[]{:T(128)}, s32[]{:T(128)}) while((s32[]{:T(128)}, f32[4,512,128]{2,1,0:T(8,128)S(1)}, f32[]{:T(128)}, s32[4,512]{1,0:T(4,128)S(1)}, ...), condition=%wide.region_7.9_spmd.clone, body=%wide.region_6.8_spmd.clone.sunk | while | flops 548472832 | bytes 1466969 | solution.py:65
  92.6 4.6 %fusion.144 = f32[4,512,128]{2,1,0:T(8,128)S(1)} fusion(f32[4,512,128]{2,1,0:T(8,128)S(1)} %get-tuple-element.965, s32[]{:T(128)} %get-tuple-element.964, bf16[2048,128]{1,0:T(8,128)(2,1)} %get-tuple-element.977, f32[]{:T(128)} %get-tuple-element.978, f32[]{:T(128)} %get-tuple-element.974, s32[2048]{0:T(1024)S(1)} %iota_add_fusion.12, ...), kind=kOutput, calls=%fused_computation.17.clone.1 | convolution fusion | flops 548470784 | bytes 1454592 | tf_op jit(solution)/shard_map/while/body/eval_jaxpr/dot_general | solution.py:63
  97.3 4.5 %fusion.144 = f32[4,512,128]{2,1,0:T(8,128)S(1)} fusion(f32[4,512,128]{2,1,0:T(8,128)S(1)} %get-tuple-element.965, s32[]{:T(128)} %get-tuple-element.964, bf16[2048,128]{1,0:T(8,128)(2,1)} %get-tuple-element.977, f32[]{:T(128)} %get-tuple-element.978, f32[]{:T(128)} %get-tuple-element.974, s32[2048]{0:T(1024)S(1)} %iota_add_fusion.12, ...), kind=kOutput, calls=%fused_computation.17.clone.1 | convolution fusion | flops 548470784 | bytes 1454592 | tf_op jit(solution)/shard_map/while/body/eval_jaxpr/dot_general | solution.py:63
  106.3 4.5 %fusion.144 = f32[4,512,128]{2,1,0:T(8,128)S(1)} fusion(f32[4,512,128]{2,1,0:T(8,128)S(1)} %get-tuple-element.965, s32[]{:T(128)} %get-tuple-element.964, bf16[2048,128]{1,0:T(8,128)(2,1)} %get-tuple-element.977, f32[]{:T(128)} %get-tuple-element.978, f32[]{:T(128)} %get-tuple-element.974, s32[2048]{0:T(1024)S(1)} %iota_add_fusion.12, ...), kind=kOutput, calls=%fused_computation.17.clone.1 | convolution fusion | flops 548470784 | bytes 1454592 | tf_op jit(solution)/shard_map/while/body/eval_jaxpr/dot_general | solution.py:63
  111.1 20.2 %while.84 = (s32[]{:T(128)}, f32[2048,128]{1,0:T(8,128)S(1)}, f32[]{:T(128)}, s32[4,512]{1,0:T(4,128)S(1)}, bf16[4,512,128]{2,1,0:T(8,128)(2,1)}, /*index=5*/bf1...) while((s32[]{:T(128)}, f32[2048,128]{1,0:T(8,128)S(1)}, f32[]{:T(128)}, ...), condition=%wide.region_20.23_spmd.clone, body=%wide.region_19.22_spmd.clone.sunk | while | flops 549193728 | bytes 2908779 | solution.py:89
  111.1 5.0 %fusion.168 = f32[2048,128]{1,0:T(8,128)S(1)} fusion(bf16[2048,128]{1,0:T(8,128)(2,1)S(1)} %get-tuple-element.1030, f32[]{:T(128)} %get-tuple-element.1031, f32[]{:T(128)} %get-tuple-element.1027, s32[2048]{0:T(1024)S(1)} %iota_add_fusion.16, s32[512]{0:T(512)S(1)} %bitcast.166, f32[2048,128]{1,0:T(8,128)S(1)} %get-tuple-element.1017, ...), kind=kOutput, calls=%fused_computation.75.clone.1 | convolution fusion | flops 549191680 | bytes 2896385 | tf_op jit(solution)/shard_map/while/body/eval_jaxpr/dot_general | solution.py:82
  116.2 5.0 %fusion.168 = f32[2048,128]{1,0:T(8,128)S(1)} fusion(bf16[2048,128]{1,0:T(8,128)(2,1)S(1)} %get-tuple-element.1030, f32[]{:T(128)} %get-tuple-element.1031, f32[]{:T(128)} %get-tuple-element.1027, s32[2048]{0:T(1024)S(1)} %iota_add_fusion.16, s32[512]{0:T(512)S(1)} %bitcast.166, f32[2048,128]{1,0:T(8,128)S(1)} %get-tuple-element.1017, ...), kind=kOutput, calls=%fused_computation.75.clone.1 | convolution fusion | flops 549191680 | bytes 2896385 | tf_op jit(solution)/shard_map/while/body/eval_jaxpr/dot_general | solution.py:82
  121.2 5.0 %fusion.168 = f32[2048,128]{1,0:T(8,128)S(1)} fusion(bf16[2048,128]{1,0:T(8,128)(2,1)S(1)} %get-tuple-element.1030, f32[]{:T(128)} %get-tuple-element.1031, f32[]{:T(128)} %get-tuple-element.1027, s32[2048]{0:T(1024)S(1)} %iota_add_fusion.16, s32[512]{0:T(512)S(1)} %bitcast.166, f32[2048,128]{1,0:T(8,128)S(1)} %get-tuple-element.1017, ...), kind=kOutput, calls=%fused_computation.75.clone.1 | convolution fusion | flops 549191680 | bytes 2896385 | tf_op jit(solution)/shard_map/while/body/eval_jaxpr/dot_general | solution.py:82
  126.3 5.0 %fusion.168 = f32[2048,128]{1,0:T(8,128)S(1)} fusion(bf16[2048,128]{1,0:T(8,128)(2,1)S(1)} %get-tuple-element.1030, f32[]{:T(128)} %get-tuple-element.1031, f32[]{:T(128)} %get-tuple-element.1027, s32[2048]{0:T(1024)S(1)} %iota_add_fusion.16, s32[512]{0:T(512)S(1)} %bitcast.166, f32[2048,128]{1,0:T(8,128)S(1)} %get-tuple-element.1017, ...), kind=kOutput, calls=%fused_computation.75.clone.1 | convolution fusion | flops 549191680 | bytes 2896385 | tf_op jit(solution)/shard_map/while/body/eval_jaxpr/dot_general | solution.py:82
  132.3 18.1 %while.80 = (s32[]{:T(128)}, f32[4,512,128]{2,1,0:T(8,128)S(1)}, f32[]{:T(128)}, s32[4,512]{1,0:T(4,128)S(1)}, bf16[4,512,128]{2,1,0:T(8,128)(2,1)S(1)}, /*index=5*/bf16[2048,128]{1,0:T(8,128)(2,1)}, f32[]{:T(128)}, s32[]{:T(128)}) while((s32[]{:T(128)}, f32[4,512,128]{2,1,0:T(8,128)S(1)}, f32[]{:T(128)}, ...), condition=%wide.region_9.11_spmd.clone, body=%wide.region_8.10_spmd.clone.sunk | while | flops 548472832 | bytes 1466969 | solution.py:65
  136.9 4.5 %fusion.148 = f32[4,512,128]{2,1,0:T(8,128)S(1)} fusion(f32[4,512,128]{2,1,0:T(8,128)S(1)} %get-tuple-element.911, s32[]{:T(128)} %get-tuple-element.910, bf16[2048,128]{1,0:T(8,128)(2,1)} %get-tuple-element.923, f32[]{:T(128)} %get-tuple-element.924, f32[]{:T(128)} %get-tuple-element.920, s32[2048]{0:T(1024)S(1)} %iota_add_fusion.13, ...), kind=kOutput, calls=%fused_computation.29.clone.1 | convolution fusion | flops 548470784 | bytes 1454592 | tf_op jit(solution)/shard_map/while/body/eval_jaxpr/dot_general | solution.py:63
  150.5 4.8 %collective-permute-start.8 = (bf16[2048,128]{1,0:T(8,128)(2,1)}, bf16[2048,128]{1,0:T(8,128)(2,1)}, u32[]{:S(2)}, u32[]{:S(2)}) collective-permute-start(bf16[2048,128]{1,0:T(8,128)(2,1)} %collective-permute-done.6), channel_id=1, source_target_pairs={{4,0},{8,4},{12,8},{16,12},{20,16},{24,20},{28,24},{0,28},{5,1},{9... | collective-permute-start | bytes 1572872 | tf_op jit(solution)/shard_map/ppermute | solution.py:15
  156.3 20.8 %while.81 = (s32[]{:T(128)}, f32[4,512,128]{2,1,0:T(8,128)}, f32[]{:T(128)}, s32[4,512]{1,0:T(4,128)S(1)}, bf16[4,512,128]{2,1,0:T(8,128)(2,1)S(1)}, /*index=5*/bf16[2048,128]{1,0:T(8,128)(2,1)}, f32[]{:T(128)}, s32[]{:T(128)}) while((s32[]{:T(128)}, f32[4,512,128]{2,1,0:T(8,128)}, f32[]{:T(128)}, s32[4,512]{1,0:T(4,128)S(1)}, ...), condition=%wide.region_11.13_spmd.clone, body=%wide.region_10.12_spmd.clone.sunk | while | flops 548472832 | bytes 1466969 | solution.py:65
  156.4 5.2 %fusion.152 = f32[4,512,128]{2,1,0:T(8,128)} fusion(f32[4,512,128]{2,1,0:T(8,128)} %get-tuple-element.887, s32[]{:T(128)} %get-tuple-element.886, bf16[2048,128]{1,0:T(8,128)(2,1)} %get-tuple-element.899, f32[]{:T(128)} %get-tuple-element.900, f32[]{:T(128)} %get-tuple-element.896, s32[2048]{0:T(1024)S(1)} %iota_add_fusion.14, ...), kind=kOutput, calls=%fused_computation.41.clone.1 | convolution fusion | flops 548470784 | bytes 1454592 | tf_op jit(solution)/shard_map/while/body/eval_jaxpr/dot_general | solution.py:63
  161.6 5.2 %fusion.152 = f32[4,512,128]{2,1,0:T(8,128)} fusion(f32[4,512,128]{2,1,0:T(8,128)} %get-tuple-element.887, s32[]{:T(128)} %get-tuple-element.886, bf16[2048,128]{1,0:T(8,128)(2,1)} %get-tuple-element.899, f32[]{:T(128)} %get-tuple-element.900, f32[]{:T(128)} %get-tuple-element.896, s32[2048]{0:T(1024)S(1)} %iota_add_fusion.14, ...), kind=kOutput, calls=%fused_computation.41.clone.1 | convolution fusion | flops 548470784 | bytes 1454592 | tf_op jit(solution)/shard_map/while/body/eval_jaxpr/dot_general | solution.py:63
  166.8 5.2 %fusion.152 = f32[4,512,128]{2,1,0:T(8,128)} fusion(f32[4,512,128]{2,1,0:T(8,128)} %get-tuple-element.887, s32[]{:T(128)} %get-tuple-element.886, bf16[2048,128]{1,0:T(8,128)(2,1)} %get-tuple-element.899, f32[]{:T(128)} %get-tuple-element.900, f32[]{:T(128)} %get-tuple-element.896, s32[2048]{0:T(1024)S(1)} %iota_add_fusion.14, ...), kind=kOutput, calls=%fused_computation.41.clone.1 | convolution fusion | flops 548470784 | bytes 1454592 | tf_op jit(solution)/shard_map/while/body/eval_jaxpr/dot_general | solution.py:63
  172.0 5.2 %fusion.152 = f32[4,512,128]{2,1,0:T(8,128)} fusion(f32[4,512,128]{2,1,0:T(8,128)} %get-tuple-element.887, s32[]{:T(128)} %get-tuple-element.886, bf16[2048,128]{1,0:T(8,128)(2,1)} %get-tuple-element.899, f32[]{:T(128)} %get-tuple-element.900, f32[]{:T(128)} %get-tuple-element.896, s32[2048]{0:T(1024)S(1)} %iota_add_fusion.14, ...), kind=kOutput, calls=%fused_computation.41.clone.1 | convolution fusion | flops 548470784 | bytes 1454592 | tf_op jit(solution)/shard_map/while/body/eval_jaxpr/dot_general | solution.py:63
  188.6 4.6 %all-to-all-start.1 = ((f32[4,8,128,128]{3,2,1,0:T(8,128)}), f32[4,8,128,128]{3,2,1,0:T(8,128)}, u32[]{:S(2)}, u32[]{:S(2)}) async-start(f32[4,8,128,128]{3,2,1,0:T(8,128)} %bitcast.8), calls=%async_computation.1 | async-start | bytes 4194304 | tf_op jit(solution)/shard_map/all_to_all | solution.py:147
  193.2 23.0 %while.85 = (s32[]{:T(128)}, f32[2048,128]{1,0:T(8,128)S(1)}, f32[]{:T(128)}, s32[4,512]{1,0:T(4,128)}, bf16[4,512,128]{2,1,0:T(8,128)(2,1)}, /*index=5*/bf16[20...) while((s32[]{:T(128)}, f32[2048,128]{1,0:T(8,128)S(1)}, f32[]{:T(128)}, ...), condition=%wide.region_22.25_spmd.clone, body=%wide.region_21.24_spmd.clone.sunk | while | flops 549193728 | bytes 2908779 | solution.py:89
  194.0 5.0 %fusion.172 = f32[2048,128]{1,0:T(8,128)S(1)} fusion(bf16[2048,128]{1,0:T(8,128)(2,1)S(1)} %get-tuple-element.1003, f32[]{:T(128)} %get-tuple-element.1004, f32[]{:T(128)} %get-tuple-element.1000, s32[2048]{0:T(1024)S(1)} %iota_add_fusion.17, s32[512]{0:T(512)S(1)} %bitcast.167, f32[2048,128]{1,0:T(8,128)S(1)} %get-tuple-element.990, ...), kind=kOutput, calls=%fused_computation.85.clone.1 | convolution fusion | flops 549191680 | bytes 2896385 | tf_op jit(solution)/shard_map/while/body/eval_jaxpr/dot_general | solution.py:82
  199.7 5.0 %fusion.172 = f32[2048,128]{1,0:T(8,128)S(1)} fusion(bf16[2048,128]{1,0:T(8,128)(2,1)S(1)} %get-tuple-element.1003, f32[]{:T(128)} %get-tuple-element.1004, f32[]{:T(128)} %get-tuple-element.1000, s32[2048]{0:T(1024)S(1)} %iota_add_fusion.17, s32[512]{0:T(512)S(1)} %bitcast.167, f32[2048,128]{1,0:T(8,128)S(1)} %get-tuple-element.990, ...), kind=kOutput, calls=%fused_computation.85.clone.1 | convolution fusion | flops 549191680 | bytes 2896385 | tf_op jit(solution)/shard_map/while/body/eval_jaxpr/dot_general | solution.py:82
  205.4 5.0 %fusion.172 = f32[2048,128]{1,0:T(8,128)S(1)} fusion(bf16[2048,128]{1,0:T(8,128)(2,1)S(1)} %get-tuple-element.1003, f32[]{:T(128)} %get-tuple-element.1004, f32[]{:T(128)} %get-tuple-element.1000, s32[2048]{0:T(1024)S(1)} %iota_add_fusion.17, s32[512]{0:T(512)S(1)} %bitcast.167, f32[2048,128]{1,0:T(8,128)S(1)} %get-tuple-element.990, ...), kind=kOutput, calls=%fused_computation.85.clone.1 | convolution fusion | flops 549191680 | bytes 2896385 | tf_op jit(solution)/shard_map/while/body/eval_jaxpr/dot_general | solution.py:82
  211.1 5.0 %fusion.172 = f32[2048,128]{1,0:T(8,128)S(1)} fusion(bf16[2048,128]{1,0:T(8,128)(2,1)S(1)} %get-tuple-element.1003, f32[]{:T(128)} %get-tuple-element.1004, f32[]{:T(128)} %get-tuple-element.1000, s32[2048]{0:T(1024)S(1)} %iota_add_fusion.17, s32[512]{0:T(512)S(1)} %bitcast.167, f32[2048,128]{1,0:T(8,128)S(1)} %get-tuple-element.990, ...), kind=kOutput, calls=%fused_computation.85.clone.1 | convolution fusion | flops 549191680 | bytes 2896385 | tf_op jit(solution)/shard_map/while/body/eval_jaxpr/dot_general | solution.py:82
  228.5 26.9 %scatter_custom_fusion = f32[1024,128]{1,0:T(8,128)} fusion(s32[4096]{0:T(1024)} %bitcast.3, f32[4096,128]{1,0:T(8,128)} %bitcast.9, f32[]{:T(128)} %constant.133.clone.1), kind=kCustom, calls=%fused_computation.99 | custom fusion | flops 524288 | bytes 524800 | tf_op jit(solution)/shard_map/scatter-add | solution.py:152
  255.4 27.8 %scatter_custom_fusion.1 = f32[1024,128]{1,0:T(8,128)} fusion(s32[4096]{0:T(1024)S(1)} %bitcast.172, f32[4096,128]{1,0:T(8,128)S(1)} %bitcast.163, f32[]{:T(128)} %constant.133.clone.1), kind=kCustom, calls=%fused_computation.97 | custom fusion | flops 524288 | bytes 524292 | tf_op jit(solution)/shard_map/scatter-add | solution.py:155
  (185 shorter events, 113.1 us)
Async XLA Ops:
  0.6 6.1 %copy-start = (s32[2048]{0:T(1024)S(1)}, s32[2048]{0:T(1024)}, u32[]{:S(2)}) copy-start(s32[2048]{0:T(1024)} %param.32) | copy-start | bytes 24580
  0.6 91.8 %collective-permute-start = (bf16[2048,128]{1,0:T(8,128)(2,1)}, bf16[2048,128]{1,0:T(8,128)(2,1)}, u32[]{:S(2)}, u32[]{:S(2)}) collective-permute-start(bf16[2048,128]{1,0:T(8,128)(2,1)} %param.28), channel_id=1, source_target_pairs={{28,0},{0,4},{4,8},{8,12},{12,16},{16,20},{20,24},{24,28},{29,1},{... | collective-permute-start | bytes 1572872 | tf_op jit(solution)/shard_map/ppermute | solution.py:15
  6.6 10.4 %copy-start.15 = (pred[32]{0:T(512)(128)(4,1)}, pred[32]{0:T(512)(128)(4,1)S(1)}, u32[]{:S(2)}) copy-start(pred[32]{0:T(512)(128)(4,1)S(1)} %compare_and_fusion.1) | copy-start | bytes 100
  6.7 10.3 %copy-start.17 = (pred[32]{0:T(512)(128)(4,1)}, pred[32]{0:T(512)(128)(4,1)S(1)}, u32[]{:S(2)}) copy-start(pred[32]{0:T(512)(128)(4,1)S(1)} %fusion.94) | copy-start | bytes 100
  6.7 10.2 %copy-start.13 = (s32[1024]{0:T(1024)}, s32[1024]{0:T(1024)S(1)}, u32[]{:S(2)}) copy-start(s32[1024]{0:T(1024)S(1)} %pad_clamp_fusion.1) | copy-start | bytes 12292
  8.0 173.5 %all-to-all-start = ((s32[4,8,128]{2,1,0:T(8,128)}), s32[4,8,128]{2,1,0:T(8,128)}, u32[]{:S(2)}, u32[]{:S(2)}) async-start(s32[4,8,128]{2,1,0:T(8,128)} %fusion.91), calls=%async_computation | async-start | bytes 32768 | tf_op jit(solution)/shard_map/all_to_all | solution.py:148
  11.8 54.9 %collective-permute-start.4 = (bf16[2048,128]{1,0:T(8,128)(2,1)}, bf16[2048,128]{1,0:T(8,128)(2,1)}, u32[]{:S(2)}, u32[]{:S(2)}) collective-permute-start(bf16[2048,128]{1,0:T(8,128)(2,1)} %param.27), channel_id=1, source_target_pairs={{4,0},{8,4},{12,8},{16,12},{20,16},{24,20},{28,24},{0,28},{5,1},{9... | collective-permute-start | bytes 1572872 | tf_op jit(solution)/shard_map/ppermute | solution.py:15
  14.9 42.0 %collective-permute-start.3 = (s32[2048]{0:T(1024)}, s32[2048]{0:T(1024)S(1)}, u32[]{:S(2)}, u32[]{:S(2)}) collective-permute-start(s32[2048]{0:T(1024)} %param.31), channel_id=1, source_target_pairs={{4,0},{8,4},{12,8},{16,12},{20,16},{24,20},{28,24},{0,28},{5,1},{9... | collective-permute-start | bytes 24584 | tf_op jit(solution)/shard_map/ppermute | solution.py:15
  18.7 37.1 %copy-start.23 = (s32[16,1]{0,1:T(1,128)S(1)}, s32[16,1]{0,1:T(1,128)}, u32[]{:S(2)}) copy-start(s32[16,1]{0,1:T(1,128)} %param.35) | copy-start | bytes 196
  18.8 39.6 %copy-start.6 = (s32[2048]{0:T(1024)S(1)}, s32[2048]{0:T(1024)}, u32[]{:S(2)}) copy-start(s32[2048]{0:T(1024)} %param.33) | copy-start | bytes 24580
  41.8 2.8 copy-start.3
  55.9 10.8 %copy-start.1 = (f32[2048,128]{1,0:T(8,128)}, f32[2048,128]{1,0:T(8,128)S(1)}, u32[]{:S(2)}) copy-start(f32[2048,128]{1,0:T(8,128)S(1)} %get-tuple-element.312) | copy-start | bytes 3145732
  56.8 9.9 %copy-start.19 = (pred[32]{0:T(512)(128)(4,1)}, pred[32]{0:T(512)(128)(4,1)S(1)}, u32[]{:S(2)}) copy-start(pred[32]{0:T(512)(128)(4,1)S(1)} %compare_and_fusion) | copy-start | bytes 100
  56.9 9.8 %copy-start.21 = (pred[32]{0:T(512)(128)(4,1)}, pred[32]{0:T(512)(128)(4,1)S(1)}, u32[]{:S(2)}) copy-start(pred[32]{0:T(512)(128)(4,1)S(1)} %fusion.92) | copy-start | bytes 100
  56.9 3.7 %collective-permute-start.5 = (s32[2048]{0:T(1024)S(1)}, s32[2048]{0:T(1024)S(1)}, u32[]{:S(2)}, u32[]{:S(2)}) collective-permute-start(s32[2048]{0:T(1024)S(1)} %collective-permute-done.3), channel_id=1, source_target_pairs={{4,0},{8,4},{12,8},{16,12},{20,16},{24,20},{28,24},{0,28},{5,1},{9... | collective-permute-start | bytes 24584 | tf_op jit(solution)/shard_map/ppermute | solution.py:15
  60.6 5.5 %collective-permute-start.7 = (s32[2048]{0:T(1024)S(1)}, s32[2048]{0:T(1024)S(1)}, u32[]{:S(2)}, u32[]{:S(2)}) collective-permute-start(s32[2048]{0:T(1024)S(1)} %collective-permute-done.5), channel_id=1, source_target_pairs={{4,0},{8,4},{12,8},{16,12},{20,16},{24,20},{28,24},{0,28},{5,1},{9... | collective-permute-start | bytes 24584 | tf_op jit(solution)/shard_map/ppermute | solution.py:15
  66.7 25.8 %copy-start.12 = (bf16[4,512,128]{2,1,0:T(8,128)(2,1)S(1)}, bf16[4,512,128]{2,1,0:T(8,128)(2,1)}, u32[]{:S(2)}) copy-start(bf16[4,512,128]{2,1,0:T(8,128)(2,1)} %get-tuple-element.1067) | copy-start | bytes 1572868
  87.4 5.0 %copy-start.11 = (f32[2048,128]{1,0:T(8,128)}, f32[2048,128]{1,0:T(8,128)S(1)}, u32[]{:S(2)}) copy-start(f32[2048,128]{1,0:T(8,128)S(1)} %get-tuple-element.313) | copy-start | bytes 3145732
  87.4 23.6 %collective-permute-start.6 = (bf16[2048,128]{1,0:T(8,128)(2,1)}, bf16[2048,128]{1,0:T(8,128)(2,1)}, u32[]{:S(2)}, u32[]{:S(2)}) collective-permute-start(bf16[2048,128]{1,0:T(8,128)(2,1)} %collective-permute-done.4), channel_id=1, source_target_pairs={{4,0},{8,4},{12,8},{16,12},{20,16},{24,20},{28,24},{0,28},{5,1},{9... | collective-permute-start | bytes 1572872 | tf_op jit(solution)/shard_map/ppermute | solution.py:15
  92.6 18.5 %copy-start.4 = (bf16[2048,128]{1,0:T(8,128)(2,1)S(1)}, bf16[2048,128]{1,0:T(8,128)(2,1)}, u32[]{:S(2)}) copy-start(bf16[2048,128]{1,0:T(8,128)(2,1)} %get-tuple-element.1063) | copy-start | bytes 1572868
  92.6 18.5 %copy-start.9 = (f32[2048,128]{1,0:T(8,128)S(1)}, f32[2048,128]{1,0:T(8,128)}, u32[]{:S(2)}) copy-start(f32[2048,128]{1,0:T(8,128)} %custom-call.2) | copy-start | bytes 3145732
  110.8 20.5 %collective-permute-start.1 = (bf16[2048,128]{1,0:T(8,128)(2,1)}, bf16[2048,128]{1,0:T(8,128)(2,1)}, u32[]{:S(2)}, u32[]{:S(2)}) collective-permute-start(bf16[2048,128]{1,0:T(8,128)(2,1)} %collective-permute-done), channel_id=1, source_target_pairs={{28,0},{0,4},{4,8},{8,12},{12,16},{16,20},{20,24},{24,28},{29,1},{... | collective-permute-start | bytes 1572872 | tf_op jit(solution)/shard_map/ppermute | solution.py:15
  132.3 23.0 %collective-permute-start.2 = (bf16[2048,128]{1,0:T(8,128)(2,1)}, bf16[2048,128]{1,0:T(8,128)(2,1)}, u32[]{:S(2)}, u32[]{:S(2)}) collective-permute-start(bf16[2048,128]{1,0:T(8,128)(2,1)} %collective-permute-done.1), channel_id=1, source_target_pairs={{28,0},{0,4},{4,8},{8,12},{12,16},{16,20},{20,24},{24,28},{29,1},{... | collective-permute-start | bytes 1572872 | tf_op jit(solution)/shard_map/ppermute | solution.py:15
  150.5 5.9 %copy-start.5 = (f32[4,512,128]{2,1,0:T(8,128)}, f32[4,512,128]{2,1,0:T(8,128)S(1)}, u32[]{:S(2)}) copy-start(f32[4,512,128]{2,1,0:T(8,128)S(1)} %get-tuple-element.309) | copy-start | bytes 3145732
  150.5 42.7 %collective-permute-start.8 = (bf16[2048,128]{1,0:T(8,128)(2,1)}, bf16[2048,128]{1,0:T(8,128)(2,1)}, u32[]{:S(2)}, u32[]{:S(2)}) collective-permute-start(bf16[2048,128]{1,0:T(8,128)(2,1)} %collective-permute-done.6), channel_id=1, source_target_pairs={{4,0},{8,4},{12,8},{16,12},{20,16},{24,20},{28,24},{0,28},{5,1},{9... | collective-permute-start | bytes 1572872 | tf_op jit(solution)/shard_map/ppermute | solution.py:15
  179.4 5.4 %copy-start.16 = (pred[32]{0:T(512)(128)(4,1)S(1)}, pred[32]{0:T(512)(128)(4,1)}, u32[]{:S(2)}) copy-start(pred[32]{0:T(512)(128)(4,1)} %copy-done.15) | copy-start | bytes 100
  179.4 5.4 %copy-start.18 = (pred[32]{0:T(512)(128)(4,1)S(1)}, pred[32]{0:T(512)(128)(4,1)}, u32[]{:S(2)}) copy-start(pred[32]{0:T(512)(128)(4,1)} %copy-done.17) | copy-start | bytes 100
  181.5 7.1 %all-to-all-start.2 = ((s32[4,8,128]{2,1,0:T(8,128)}), s32[4,8,128]{2,1,0:T(8,128)S(1)}, u32[]{:S(2)}, u32[]{:S(2)}) async-start(s32[4,8,128]{2,1,0:T(8,128)} %fusion.90), calls=%async_computation.2 | async-start | bytes 32768 | tf_op jit(solution)/shard_map/all_to_all | solution.py:150
  188.6 4.6 %copy-start.7 = (f32[2048,128]{1,0:T(8,128)S(1)}, f32[2048,128]{1,0:T(8,128)}, u32[]{:S(2)}) copy-start(f32[2048,128]{1,0:T(8,128)} %custom-call.3) | copy-start | bytes 3145732
  188.6 36.1 %all-to-all-start.1 = ((f32[4,8,128,128]{3,2,1,0:T(8,128)}), f32[4,8,128,128]{3,2,1,0:T(8,128)}, u32[]{:S(2)}, u32[]{:S(2)}) async-start(f32[4,8,128,128]{3,2,1,0:T(8,128)} %bitcast.8), calls=%async_computation.1 | async-start | bytes 4194304 | tf_op jit(solution)/shard_map/all_to_all | solution.py:147
  193.2 24.0 %copy-start.2 = (f32[2048,128]{1,0:T(8,128)S(1)}, f32[2048,128]{1,0:T(8,128)}, u32[]{:S(2)}) copy-start(f32[2048,128]{1,0:T(8,128)} %copy-done.1) | copy-start | bytes 3145732
  224.7 30.7 %all-to-all-start.3 = ((f32[4,8,128,128]{3,2,1,0:T(8,128)}), f32[4,8,128,128]{3,2,1,0:T(8,128)S(1)}, u32[]{:S(2)}, u32[]{:S(2)}) async-start(f32[4,8,128,128]{3,2,1,0:T(8,128)} %bitcast.18), calls=%async_computation.3 | async-start | bytes 4194304 | tf_op jit(solution)/shard_map/all_to_all | solution.py:149
  (8 other events, 15.1 us)
where the time goes:
time: 286 us; the launch traced here: 283 us
  matrix products  154 us (54%)
  other arithmetic  70.9 us (25%)
  starting transfers between devices  39.3 us (14%)
  local copies, waits for them, and re-layouts  14.2 us (5%)
  waiting for transfers between devices  2.94 us (1%)
    dot_general x12, matrix products, merchant_one_block(): lax.dot_general(delta, piece, (((0,), (0,)), ((), ())), preferred_element...  60.4 us
    dot_general x12, matrix products, account_one_block(): jnp.dot(delta, merch_block, preferred_element_type=jnp.float32)  56.7 us
    scatter-add x1, other arithmetic, per_device(): jax.ops.segment_sum(merch_payload.reshape(-1, D), merch_keys.reshape(-1),...  27.8 us
    scatter-add x1, other arithmetic, per_device(): jax.ops.segment_sum(acc_payload.reshape(-1, D), acc_keys.reshape(-1), num...  26.9 us
    ppermute x9, starting transfers between devices, shifted(): return lax.ppermute(block, axis, route)  23.8 us
    dot_general x4, matrix products, score_delta(): lax.dot_general(piece, merch_block, (((1,), (1,)), ((), ())), preferred_e...  17.7 us
    dot_general x4, matrix products, tile_one_block(): lax.dot_general(delta, piece, (((0,), (0,)), ((), ())), preferred_element...  10.9 us
    dot_general x4, matrix products, tile_one_block(): jnp.dot(delta, merch_block, preferred_element_type=jnp.float32)  8.3 us
  transfers between devices with their start and end apart: 13, of which 3 were waited for; matrix products, arithmetic and copies ran while one was open for 74% of the time, Pallas kernels for 0%

commit v1 on v0

v1 whole, which is shorter than its diff:
```python
import functools

import jax
import jax.numpy as jnp
from jax import lax
from jax.experimental import pallas as pl
from jax.experimental.pallas import tpu as pltpu
from jax.sharding import PartitionSpec as P

STEPS = 4
BLOCK_ROWS = 128
TROWS = 1024
ROW_STEP = 512
COL_STEP = 512
MESH = pl.DeviceIdType.MESH


def kernel(
    n_blk,
    acc_in, merch_in, pos_in, acc_ids, merch_ids, acc_own, merch_own, scale_in, bias_in,
    acc_out, merch_out,
    guests_m, guests_a, guests_l, label_cols, grad_a, grad_m, split_a, split_m, keys_a, keys_m,
    pair_send, pair_recv, far_send, far_recv,
    send_m, recv_m, send_a, recv_a, send_l, recv_l,
    pair_ssem, pair_rsem, far_ssem, far_rsem,
):
    rows, width = acc_in.shape
    blocks = rows // BLOCK_ROWS
    row_step, col_step = min(ROW_STEP, rows), min(COL_STEP, rows)
    i, k = lax.axis_index("blk"), lax.axis_index("tab")
    odd = lax.rem(i, 2)
    even = 1 - odd
    up, down = lax.rem(i + 2, n_blk), lax.rem(i + n_blk - 2, n_blk)
    beside = i + 1 - 2 * odd
    core_bit, far_bit = lax.rem(k, 2), k // 2
    pair = far_bit * 2 + 1 - core_bit
    far = (1 - far_bit) * 2 + core_bit
    cross = (1 - far_bit) * 2 + 1 - core_bit
    half_scale = scale_in[0] * 0.5
    half_bias = bias_in[0] * 0.5

    barrier = pltpu.get_barrier_semaphore()
    for there in ((up, k), (down, k), (beside, k), (i, pair), (i, far)):
        pl.semaphore_signal(barrier, inc=1, device_id=there, device_id_type=MESH)
    pl.semaphore_wait(barrier, 5)

    def send(src, dst, ssem, rsem, there):
        return pltpu.make_async_remote_copy(
            src_ref=src, dst_ref=dst, send_sem=ssem, recv_sem=rsem, device_id=there, device_id_type=MESH
        )

    def merch_copy(src, hop, slot, there):
        return (send(src, guests_m.at[slot], send_m.at[hop], recv_m.at[slot], there),)

    def acc_copy(src, labels, hop, slot, there):
        return (
            send(src, guests_a.at[slot], send_a.at[hop], recv_a.at[slot], there),
            send(labels, guests_l.at[slot], send_l.at[hop], recv_l.at[slot], there),
        )

    def start(copies):
        for copy in copies:
            copy.start()

    m_hops = (
        merch_copy(merch_in, 0, 1, (up, k)),
        merch_copy(merch_in, 1, 0, (beside, k)),
        merch_copy(guests_m.at[1], 2, 2 * even, (beside, k)),
        merch_copy(guests_m.at[0], 3, 2, (up, k)),
    )
    a_hops = (
        acc_copy(acc_in, pos_in, 0, 1, (down, k)),
        acc_copy(acc_in, pos_in, 1, 0, (beside, k)),
        acc_copy(guests_a.at[1], guests_l.at[1], 2, 2 * odd, (beside, k)),
        acc_copy(guests_a.at[0], guests_l.at[0], 3, 2, (down, k)),
    )

    def arrived_m(slot):
        send(guests_m.at[slot], guests_m.at[slot], send_m.at[0], recv_m.at[slot], (up, k)).wait_recv()

    def arrived_a(slot):
        send(guests_a.at[slot], guests_a.at[slot], send_a.at[0], recv_a.at[slot], (up, k)).wait_recv()
        send(guests_l.at[slot], guests_l.at[slot], send_l.at[0], recv_l.at[slot], (up, k)).wait_recv()

    start(m_hops[0])
    start(a_hops[0])

    @pl.when(odd == 0)
    def _():
        start(m_hops[1])

    @pl.when(odd == 1)
    def _():
        start(a_hops[1])

    for block in range(blocks):
        column = jnp.broadcast_to(pos_in[block : block + 1, :], (BLOCK_ROWS, BLOCK_ROWS)).T
        label_cols[block * BLOCK_ROWS : (block + 1) * BLOCK_ROWS, :] = column
    keys_a[...] = acc_own[...] * TROWS + acc_ids[...]
    keys_m[...] = merch_own[...] * TROWS + merch_ids[...]

    def flat(ref, first, count):
        return jnp.concatenate([ref[first + j : first + j + 1, :] for j in range(count)], axis=1)

    def delta_of(mine, theirs, hit):
        logits = lax.dot_general(mine, theirs, (((1,), (1,)), ((), ())), preferred_element_type=jnp.float32)
        raised = jnp.tanh(logits * half_scale + half_bias)
        return (raised + jnp.where(hit, jnp.float32(-1.0), jnp.float32(1.0))).astype(jnp.bfloat16)

    def tile(mine, theirs, grad, first, hits):
        def piece(p, carry):
            at = pl.multiple_of(p * row_step, row_step)
            own = mine[pl.ds(at, row_step), :]
            total = jnp.zeros((row_step, width), jnp.float32)
            for c in range(0, rows, col_step):
                other = theirs[pl.ds(c, col_step), :]
                total = total + jnp.dot(
                    delta_of(own, other, hits(at, c)), other, preferred_element_type=jnp.float32
                )
            if first:
                grad[pl.ds(at, row_step), :] = total
            else:
                grad[pl.ds(at, row_step), :] += total
            return carry

        lax.fori_loop(0, rows // row_step, piece, 0)

    def acc_tile(s):
        lane = lax.broadcasted_iota(jnp.int32, (row_step, col_step), 1)

        def hits(at, c):
            labels = label_cols[pl.ds(at, row_step), :] - (s * rows + c)
            return jnp.concatenate([labels] * (col_step // BLOCK_ROWS), axis=1) == lane

        tile(acc_in, merch_in if s == 0 else guests_m.at[s - 1], grad_a, s == 0, hits)

    def merch_tile(s):
        row = lax.broadcasted_iota(jnp.int32, (row_step, col_step), 0)
        labels = pos_in if s == 0 else guests_l.at[s - 1]

        def hits(at, c):
            line = flat(labels, c // BLOCK_ROWS, col_step // BLOCK_ROWS) - (s * rows + at)
            return line == row

        tile(merch_in, acc_in if s == 0 else guests_a.at[s - 1], grad_m, s == 0, hits)

    def split(grad, pieces):
        def one(p, carry):
            at = pl.multiple_of(p * 256, 256)
            value = grad[pl.ds(at, 256), :] * half_scale
            high = value.astype(jnp.bfloat16)
            pieces[pl.ds(at, 256), 0:width] = high
            pieces[pl.ds(at, 256), width : 2 * width] = (value - high.astype(jnp.float32)).astype(jnp.bfloat16)
            return carry

        lax.fori_loop(0, rows // 256, one, 0)

    def table(pieces, keys, owner, put):
        step = 512

        def one(p, carry):
            at = pl.multiple_of(p * step, step)
            total = jnp.zeros((step, 2 * width), jnp.float32)
            row = lax.broadcasted_iota(jnp.int32, (step, col_step), 0)
            for c in range(0, rows, col_step):
                line = flat(keys, c // BLOCK_ROWS, col_step // BLOCK_ROWS) - (owner * TROWS + at)
                named = jnp.where(line == row, jnp.float32(1.0), jnp.float32(0.0)).astype(jnp.bfloat16)
                total = total + jnp.dot(
                    named, pieces[pl.ds(c, col_step), :], preferred_element_type=jnp.float32
                )
            put(pl.ds(at, step), total[:, 0:width] + total[:, width : 2 * width])
            return carry

        lax.fori_loop(0, TROWS // step, one, 0)

    def storing(ref):
        def put(at, value):
            ref[at, :] = value

        return put

    def pair_copy(side, turn):
        return send(
            pair_send.at[side, turn], pair_recv.at[side, turn], pair_ssem.at[side, turn],
            pair_rsem.at[side, turn], (i, pair),
        )

    def far_copy(side):
        return send(far_send.at[side], far_recv.at[side], far_ssem.at[side], far_rsem.at[side], (i, far))

    def give(side, pieces, keys):
        table(pieces, keys, cross, storing(pair_send.at[side, 0]))
        pair_copy(side, 0).start()
        table(pieces, keys, far, storing(far_send.at[side]))
        pair_copy(side, 0).wait_recv()
        far_send[side] = far_send[side] + pair_recv[side, 0]
        far_copy(side).start()

    acc_tile(0)
    merch_tile(0)
    arrived_m(1)
    start(m_hops[2])
    arrived_a(1)
    start(a_hops[2])
    acc_tile(2)
    merch_tile(2)
    arrived_m(0)

    @pl.when(odd == 0)
    def _():
        start(m_hops[3])

    arrived_a(0)

    @pl.when(odd == 1)
    def _():
        start(a_hops[3])

    acc_tile(1)
    merch_tile(1)
    arrived_m(2)
    acc_tile(3)
    split(grad_a, split_a)
    give(0, split_a, keys_a)
    arrived_a(2)
    merch_tile(3)
    split(grad_m, split_m)
    give(1, split_m, keys_m)
    sides = ((0, split_a, keys_a, acc_out), (1, split_m, keys_m, merch_out))
    for side, pieces, keys, out in sides:
        table(pieces, keys, pair, storing(pair_send.at[side, 1]))
        pair_copy(side, 1).start()
    for side, pieces, keys, out in sides:
        table(pieces, keys, k, storing(out))
    for side, pieces, keys, out in sides:
        pair_copy(side, 1).wait_recv()
        far_copy(side).wait_recv()
        out[...] = out[...] + pair_recv[side, 1] + far_recv[side]
        pair_copy(side, 0).wait_send()
        pair_copy(side, 1).wait_send()
        far_copy(side).wait_send()

    def drain(copies):
        for copy in copies:
            copy.wait_send()

    drain(m_hops[0] + m_hops[2] + a_hops[0] + a_hops[2])

    @pl.when(odd == 0)
    def _():
        drain(m_hops[1] + m_hops[3])

    @pl.when(odd == 1)
    def _():
        drain(a_hops[1] + a_hops[3])


def per_device(
    n_blk, accounts, merchants, logit_scale, logit_bias, positive,
    account_ids, merchant_ids, account_owner, merchant_owner,
):
    rows, width = accounts.shape
    blocks = rows // BLOCK_ROWS
    vmem = pl.BlockSpec(memory_space=pltpu.VMEM)
    smem = pl.BlockSpec(memory_space=pltpu.SMEM)
    guests = STEPS - 1
    table = jax.ShapeDtypeStruct((TROWS, width), jnp.float32)
    grid_of = lambda x: x.reshape(blocks, BLOCK_ROWS)
    return pl.pallas_call(
        functools.partial(kernel, n_blk),
        out_shape=(table, table),
        in_specs=[vmem] * 7 + [smem] * 2,
        out_specs=(vmem, vmem),
        scratch_shapes=[
            pltpu.VMEM((guests, rows, width), jnp.bfloat16),
            pltpu.VMEM((guests, rows, width), jnp.bfloat16),
            pltpu.VMEM((guests, blocks, BLOCK_ROWS), jnp.int32),
            pltpu.VMEM((rows, BLOCK_ROWS), jnp.int32),
            pltpu.VMEM((rows, width), jnp.float32),
            pltpu.VMEM((rows, width), jnp.float32),
            pltpu.VMEM((rows, 2 * width), jnp.bfloat16),
            pltpu.VMEM((rows, 2 * width), jnp.bfloat16),
            pltpu.VMEM((blocks, BLOCK_ROWS), jnp.int32),
            pltpu.VMEM((blocks, BLOCK_ROWS), jnp.int32),
            pltpu.VMEM((2, 2, TROWS, width), jnp.float32),
            pltpu.VMEM((2, 2, TROWS, width), jnp.float32),
            pltpu.VMEM((2, TROWS, width), jnp.float32),
            pltpu.VMEM((2, TROWS, width), jnp.float32),
            pltpu.SemaphoreType.DMA((4,)),
            pltpu.SemaphoreType.DMA((guests,)),
            pltpu.SemaphoreType.DMA((4,)),
            pltpu.SemaphoreType.DMA((guests,)),
            pltpu.SemaphoreType.DMA((4,)),
            pltpu.SemaphoreType.DMA((guests,)),
            pltpu.SemaphoreType.DMA((2, 2)),
            pltpu.SemaphoreType.DMA((2, 2)),
            pltpu.SemaphoreType.DMA((2,)),
            pltpu.SemaphoreType.DMA((2,)),
        ],
        compiler_params=pltpu.CompilerParams(
            collective_id=0, has_side_effects=True, vmem_limit_bytes=60 * 1024 * 1024
        ),
        name="two_tower",
    )(
        accounts, merchants, grid_of(positive), grid_of(account_ids), grid_of(merchant_ids),
        account_owner, merchant_owner, logit_scale, logit_bias,
    )


def solution(mesh):
    return jax.shard_map(
        functools.partial(per_device, mesh.shape["blk"]),
        mesh=mesh,
        in_specs=(
            P(("blk", "tab"), None),
            P(("blk", "tab"), None),
            P(),
            P(),
            P(("blk", "tab")),
            P(("blk", "tab")),
            P(("blk", "tab")),
            P(("blk", "tab"), None),
            P(("blk", "tab"), None),
        ),
        out_specs=(P(("blk", "tab"), None), P(("blk", "tab"), None)),
        check_vma=False,
    )
```

time: 286 us -> 100 us (0.35)
  matrix products: 154 us -> 0 us
  Pallas kernels: 0 us -> 93.3 us
  other arithmetic: 70.9 us -> 0 us
  starting transfers between devices: 39.3 us -> 0 us
  local copies, waits for them, and re-layouts: 14.2 us -> 4.73 us
  waiting for transfers between devices: 2.94 us -> 0 us
    dot_general x36 -> x0, matrix products: 154 us -> none  [the longest x12 60.4 us: merchant_one_block(): lax.dot_general(delta, piece, (((0,), (0,)), ((), ())), preferred_element...]
    pallas_call x0 -> x1, Pallas kernels: none -> 93.3 us  [per_device(): pl.pallas_call(functools.partial(kernel, n_blk), out_shape=(table, table)...]
    scatter-add x2 -> x0, other arithmetic: 54.7 us -> none  [the longest x1 27.8 us: per_device(): jax.ops.segment_sum(merch_payload.reshape(-1, D), merch_keys.reshape(-1),...]
    ppermute x9 -> x0, starting transfers between devices: 23.8 us -> none  [shifted(): return lax.ppermute(block, axis, route)]
    all_to_all x4 -> x0, starting transfers between devices: 15.5 us -> none  [the longest x1 4.58 us: per_device(): lax.all_to_all(acc_payload, 'tab', split_axis=0, concat_axis=0, tiled=True)]
    select_n x4 -> x0, other arithmetic: 6.4 us -> none  [the longest x2 6.4 us: pack_blocks(): payload = jnp.where(filled[:, None, None], payload, jnp.float32(0.0))]
    gather x4 -> x0, local copies, waits for them, and re-layouts: 5.38 us -> none  [the longest x2 4.23 us: pack_blocks(): jnp.take(grads.reshape(block_count, BLOCK_ROWS, D), source, axis=0)]
    add x28 -> x0, other arithmetic: 5.14 us -> none  [the longest x1 2.18 us: per_device(): acc_grad + account_only(accounts, visiting, positive, cycle_step * row_co...]
  transfers between devices with their start and end apart: 13 -> 0, of which waited for: 3 -> 0; matrix products, arithmetic and copies ran while one was open for 74% -> 0% of each run, Pallas kernels for 0% -> 0%
where the time goes in v1:
time: 100 us
  Pallas kernels  93.3 us (93%)
  local copies, waits for them, and re-layouts  4.73 us (5%)
  between operations  1.95 us (2%)
    pallas_call x1, Pallas kernels, per_device(): pl.pallas_call(functools.partial(kernel, n_blk), out_shape=(table, table)...  93.3 us
    unnamed x10, local copies, waits for them, and re-layouts  4.73 us

profile of v1, /device:TPU:0, one launch (start us, length us, event | category | flops | bytes accessed | tf_op | source)
XLA Modules:
  0.0 100.0 jit_solution(12820371282450939452)
XLA Ops:
  1.9 0.0 copy-start.1
  1.9 0.6 copy-done.1
  2.6 0.0 copy-start.2
  2.6 0.7 copy.11.acc_own
  3.3 0.0 copy-done.2
  3.3 0.7 copy.12.merch_own
  3.9 93.3 %two_tower.1 = (f32[1024,128]{1,0:T(8,128)}, f32[1024,128]{1,0:T(8,128)}) custom-call(bf16[2048,128]{1,0:T(8,128)(2,1)} %acc_in.1, bf16[2048,128]{1,0:T(8,128)(2,1)} %merch_in.1, s32[16,128]{1,0:T(8,128)} %bitcast.3, s32[16,128]{1,0:T(8,128)} %bitcast.4, s32[16,128]{1,0:T(8,128)} %bitcast.5, s32[16,1]{1,0:T(8,128)} %copy.11.acc_own, ...), custom_call_target="tpu_custom_call" | custom-call | tf_op jit(solution)/shard_map/two_tower/pallas_call | solution.py:269
  97.3 0.0 copy-start
  97.3 1.9 %copy.17 = f32[1024,128]{1,0:T(8,128)} copy(f32[1024,128]{1,0:T(8,128)} %get-tuple-element.4) | data formatting | bytes 1048576
  99.2 0.0 copy-done
  99.2 0.8 copy.18
Async XLA Ops:
  1.9 0.7 copy-start.1
  2.6 0.7 copy-start.2
  97.3 1.9 %copy-start = (f32[1024,128]{1,0:T(8,128)S(1)}, f32[1024,128]{1,0:T(8,128)}, u32[]{:S(2)}) copy-start(f32[1024,128]{1,0:T(8,128)} %get-tuple-element.5) | copy-start | bytes 1572868
